TPU v7x, 32 devices: a whole 2x2x4 slice. The times are simulated.
32 devices in a mesh: leaf: 8 (over z, y), rows: 4 (over x, core).
Axes of the slice: x: 2, y: 2, z: 4, core: 2. Of those that a mesh axis runs over, the one named last changes fastest.
Arguments:
- factor_zero: bfloat16 [4096, 4096], P('leaf', 'rows'), may hold values from -1 to 3, as said below
- factor_one: bfloat16 [8192, 4096], P('leaf', 'rows'), may hold values from -1 to 3, as said below
- factor_two: bfloat16 [16384, 4096], P('leaf', 'rows'), may hold values from -1 to 3, as said below
- factor_three: bfloat16 [32768, 4096], P('leaf', 'rows'), may hold values from -1 to 3, as said below
- coupling_one: bfloat16 [8192, 1, 4096], P('leaf', None, 'rows'), may hold values from -0.046875 to 0.046875
- coupling_two: bfloat16 [16384, 2, 4096], P('leaf', None, 'rows'), may hold values from -0.046875 to 0.046875
- coupling_three: bfloat16 [32768, 3, 4096], P('leaf', None, 'rows'), may hold values from -0.046875 to 0.046875
- noise_zero: bfloat16 [4096, 128], P('leaf'), may hold values from -6 to 6
- noise_one: bfloat16 [8192, 128], P('leaf'), may hold values from -6 to 6
- noise_two: bfloat16 [16384, 128], P('leaf'), may hold values from -6 to 6
- noise_three: bfloat16 [32768, 128], P('leaf'), may hold values from -6 to 6
- tail_index: int32 [16], replicated, may hold values from 0 to 127
Outputs:
- grad_zero: float32 [4096, 128], P('leaf')
- grad_one: float32 [8192, 128], P('leaf')
- grad_two: float32 [16384, 128], P('leaf')
- grad_three: float32 [32768, 128], P('leaf')
- tail_loss: float32 [], replicated
Inputs may be any that keep to these rules, and one draw needn't show every extreme that they name: `factor_zero`: each 4096 x 4096 node block is lower triangular with a positive diagonal. `factor_one`: each 4096 x 4096 node block is lower triangular with a positive diagonal. `factor_two`: each 4096 x 4096 node block is lower triangular with a positive diagonal. `factor_three`: each 4096 x 4096 node block is lower triangular with a positive diagonal.
All inputs are finite; a program needn't handle non-finite values.
Results may differ from a plain program's by a relative error of at most 0.008.
Values sent between devices are 32-bit elements; how exact they have to be, the bound alone decides.
No kernel may reach another device: no remote copies, remote signals or barrier semaphores. Data moves between devices by JAX's collectives and lax.ppermute only.
A program may use at most 192 MiB of HBM per device.

v0:
```python
import jax
import jax.numpy as jnp
from jax import lax
from jax.sharding import PartitionSpec as P

LEVELS = 4
tail_level = 0.5


def swapped(x, axis, apart):
    return lax.ppermute(x, axis, [(i, i ^ 1 << apart) for i in range(lax.axis_size(axis))])


def halve_bits(partial_value, bit_count, leaf_index):
    for position in range(bit_count):
        half_rows = partial_value.shape[0] // 2
        upper_bit = leaf_index >> position & 1
        kept_half = lax.dynamic_slice_in_dim(partial_value, upper_bit * half_rows, half_rows, 0)
        sent_half = lax.dynamic_slice_in_dim(
            partial_value, (1 - upper_bit) * half_rows, half_rows, 0
        )
        partial_value = kept_half + swapped(sent_half, "leaf", position)
    return partial_value


def double_bits(partial_value, bit_count, leaf_index):
    for position in reversed(range(bit_count)):
        partner = swapped(partial_value, "leaf", position)
        upper_bit = leaf_index >> position & 1
        partial_value = jnp.where(
            upper_bit == 1,
            jnp.concatenate([partner, partial_value], axis=0),
            jnp.concatenate([partial_value, partner], axis=0),
        )
    return partial_value


def group_sum(partial_value, group_bits, leaf_index):
    halved_bits = min(2, group_bits)
    partial_value = halve_bits(partial_value, halved_bits, leaf_index)
    for position in range(halved_bits, group_bits):
        partial_value = partial_value + swapped(partial_value, "leaf", position)
    return double_bits(partial_value, halved_bits, leaf_index)


def on_device(
    factor_zero,
    factor_one,
    factor_two,
    factor_three,
    coupling_one,
    coupling_two,
    coupling_three,
    noise_zero,
    noise_one,
    noise_two,
    noise_three,
    tail_index,
):
    factors = [factor_zero, factor_one, factor_two, factor_three]
    couplings = [None, coupling_one, coupling_two, coupling_three]
    noises = [noise_zero, noise_one, noise_two, noise_three]
    leaf_bits = lax.axis_size("leaf").bit_length() - 1
    leaf_index = lax.axis_index("leaf")
    full_width = factor_zero.shape[1] * lax.axis_size("rows")
    scenario_count = noise_zero.shape[1]
    columns = jnp.arange(scenario_count, dtype=jnp.int32)
    counts = jnp.sum((tail_index[:, None] == columns[None, :]).astype(jnp.float32), axis=0)
    weights = 1.0 + counts
    contract_rows = (((0,), (0,)), ((), ()))
    rounded = []
    cotangents = []
    loss_sum = jnp.float32(0.0)
    for tree_level in range(LEVELS):
        group_bits = leaf_bits - tree_level
        right_side = noises[tree_level].astype(jnp.float32)
        if tree_level > 0:
            coupling = couplings[tree_level]
            flat_coupling = coupling.reshape(
                coupling.shape[0], coupling.shape[1] * coupling.shape[2]
            )
            stacked = jnp.concatenate(rounded, axis=0)
            ancestor_terms = jnp.dot(flat_coupling, stacked, preferred_element_type=jnp.float32)
            right_side = right_side - lax.psum(ancestor_terms, "rows")
        right_round = right_side.astype(jnp.bfloat16)
        partial_sample = lax.dot_general(
            factors[tree_level], right_round, contract_rows, preferred_element_type=jnp.float32
        )
        sample = group_sum(partial_sample, group_bits, leaf_index)
        rounded.append(sample.astype(jnp.bfloat16))
        shifted = sample - tail_level
        cotangents.append(weights[None, :] * jax.nn.sigmoid(shifted))
        piece_rows = sample.shape[0] >> group_bits
        member = leaf_index & (1 << group_bits) - 1
        own_rows = lax.dynamic_slice_in_dim(shifted, member * piece_rows, piece_rows, 0)
        loss_sum = loss_sum + jnp.sum(weights[None, :] * jax.nn.softplus(own_rows))
    loss_total = lax.psum(loss_sum, ("leaf", "rows"))
    tail_loss = loss_total / jnp.float32(
        (2**LEVELS - 1) * full_width * (scenario_count + tail_index.shape[0])
    )
    pending = [jnp.zeros_like(cotangents[0]) for tree_level in range(LEVELS - 1)]
    gradients = [None] * LEVELS
    for tree_level in reversed(range(LEVELS)):
        group_bits = leaf_bits - tree_level
        if tree_level == LEVELS - 1:
            adjoint = cotangents[tree_level]
        else:
            adjoint = cotangents[tree_level] - group_sum(
                pending[tree_level], group_bits, leaf_index
            )
        adjoint_round = adjoint.astype(jnp.bfloat16)
        solved_terms = jnp.dot(
            factors[tree_level], adjoint_round, preferred_element_type=jnp.float32
        )
        solved_exact = lax.psum(solved_terms, "rows")
        gradients[tree_level] = solved_exact
        if tree_level > 0:
            solved = solved_exact.astype(jnp.bfloat16)
            upward = lax.dot_general(
                couplings[tree_level], solved, contract_rows, preferred_element_type=jnp.float32
            )
            for ancestor in range(tree_level):
                pending[ancestor] = pending[ancestor] + upward[ancestor]
    return (gradients[0], gradients[1], gradients[2], gradients[3], tail_loss)


def solution(mesh):
    in_specs = (
        P("leaf", "rows"),
        P("leaf", "rows"),
        P("leaf", "rows"),
        P("leaf", "rows"),
        P("leaf", None, "rows"),
        P("leaf", None, "rows"),
        P("leaf", None, "rows"),
        P("leaf", None),
        P("leaf", None),
        P("leaf", None),
        P("leaf", None),
        P(),
    )
    out_specs = (P("leaf", None), P("leaf", None), P("leaf", None), P("leaf", None), P())
    return jax.shard_map(
        on_device, mesh=mesh, in_specs=in_specs, out_specs=out_specs, check_vma=False
    )
```

profile of v0, /device:TPU:0, one launch (start us, length us, event | category | flops | bytes accessed | tf_op | source)
XLA Modules:
  0.0 573.5 jit_solution(12728967420345723945)
XLA Ops:
  7.2 1.8 fusion.81
  9.1 3.0 collective-permute-start
  12.1 6.3 %collective-permute-done = f32[512,128]{1,0:T(8,128)S(1)} collective-permute-done((f32[512,128]{1,0:T(8,128)S(1)}, f32[512,128]{1,0:T(8,128)S(1)}, u32[]{:S(2)}, u32[]{:S(2)}) %collective-permute-start) | collective-permute-done | bytes 262176 | tf_op jit(solution)/shard_map/ppermute | solution.py:11
  18.5 1.9 collective-permute-start.1
  20.4 3.2 collective-permute-done.1
  23.6 2.7 collective-permute-start.2
  26.3 4.7 collective-permute-done.2
  31.7 4.3 collective-permute-done.3
  37.9 4.6 collective-permute-done.4
  42.6 3.3 fusion.9
  46.1 34.3 %all-reduce.8.cloned.1.call-done = f32[1024,128]{0,1:T(8,128)} async-done(((f32[1024,128]{0,1:T(8,128)}), f32[1024,128]{0,1:T(8,128)}) %all-reduce.8.cloned.1.call-update) | async-done | bytes 524304 | tf_op jit(solution)/shard_map/psum | solution.py:84
  80.4 2.0 fusion.50
  83.9 5.4 collective-permute-done.5
  91.2 3.7 collective-permute-done.6
  94.9 1.8 collective-permute-start.7
  96.7 3.2 collective-permute-done.7
  101.8 10.1 %copy.67 = bf16[256,8,2,1024]{3,1,2,0:T(8,128)(2,1)} copy(bf16[256,8,2,1024]{3,2,1,0:T(2,128)(2,1)} %bitcast.79) | data formatting | bytes 16777216
  112.0 7.3 %convolution_bitcast_fusion.2 = f32[2048,128]{0,1:T(8,128)} fusion(bf16[2048,2048]{1,0:T(8,128)(2,1)} %bitcast.78, bf16[1024,128]{1,0:T(8,128)(2,1)S(1)} %fusion.44, bf16[1024,128]{1,0:T(8,128)(2,1)S(1)} %fusion.45), kind=kOutput, calls=%fused_computation.4 | convolution fusion | flops 1074790400 | bytes 9961472 | tf_op jit(solution)/shard_map/dot_general | solution.py:83
  120.8 33.8 %all-reduce.10.cloned.1.call-done = f32[2048,128]{0,1:T(8,128)} async-done(((f32[2048,128]{0,1:T(8,128)}), f32[2048,128]{0,1:T(8,128)}) %all-reduce.10.cloned.1.call-update) | async-done | bytes 1048592 | tf_op jit(solution)/shard_map/psum | solution.py:84
  154.6 4.2 fusion.26
  160.5 6.4 %collective-permute-done.9 = f32[512,128]{1,0:T(8,128)S(1)} collective-permute-done((f32[512,128]{1,0:T(8,128)S(1)}, f32[512,128]{1,0:T(8,128)S(1)}, u32[]{:S(2)}, u32[]{:S(2)}) %collective-permute-start.9) | collective-permute-done | bytes 262176 | tf_op jit(solution)/shard_map/ppermute | solution.py:11
  168.2 33.4 %copy.51 = bf16[4096,3,1024]{0,2,1:T(8,128)(2,1)} copy(bf16[4096,3,1024]{2,0,1:T(8,128)(2,1)} %param.18) | data formatting | bytes 50331648 | tf_op args[6]
  202.6 12.9 %convolution_bitcast_fusion.1 = f32[4096,128]{0,1:T(8,128)} fusion(bf16[4096,3072]{0,1:T(8,128)(2,1)} %bitcast.77, bf16[1024,128]{1,0:T(8,128)(2,1)S(1)} %fusion.42, bf16[1024,128]{1,0:T(8,128)(2,1)S(1)} %fusion.44, bf16[1024,128]{1,0:T(8,128)(2,1)S(1)} %fusion.45), kind=kOutput, calls=%fused_computation.3 | convolution fusion | flops 3223584768 | bytes 28049408 | tf_op jit(solution)/shard_map/dot_general | solution.py:83
  217.2 49.7 %all-reduce.12.cloned.1.call-done = f32[4096,128]{0,1:T(8,128)} async-done(((f32[4096,128]{0,1:T(8,128)}), f32[4096,128]{0,1:T(8,128)}) %all-reduce.12.cloned.1.call-update) | async-done | bytes 2097168 | tf_op jit(solution)/shard_map/psum | solution.py:84
  266.9 7.4 %fusion.28 = (f32[]{:T(128)}, f32[1024,128]{1,0:T(8,128)S(1)}) fusion(f32[128]{0:T(128)S(1)} %broadcast_add_fusion, bf16[4096,1024]{1,0:T(8,128)(2,1)} %param.15, f32[4096,128]{0,1:T(8,128)} %all-reduce.12.cloned.1.call-done, bf16[4096,128]{0,1:T(8,128)(2,1)S(1)} %copy.44), kind=kOutput, calls=%fused_computation.32 | convolution fusion | flops 1076494336 | bytes 12059140 | tf_op jit(solution)/shard_map/dot_general | solution.py:86
  274.3 7.6 %convolution_bitcast_fusion = f32[4096,128]{0,1:T(8,128)} fusion(bf16[4096,1024]{1,0:T(8,128)(2,1)} %param.15, f32[1024,128]{1,0:T(8,128)S(1)} %get-tuple-element.21, f32[128]{0:T(128)S(1)} %broadcast_add_fusion), kind=kOutput, calls=%fused_computation.2 | convolution fusion | flops 1074397184 | bytes 11010560 | tf_op jit(solution)/shard_map/dot_general | solution.py:112
  282.3 51.3 %all-reduce.14.cloned.1.call-done = f32[4096,128]{0,1:T(8,128)} async-done(((f32[4096,128]{0,1:T(8,128)}), f32[4096,128]{0,1:T(8,128)}) %all-reduce.14.cloned.1.call-update) | async-done | bytes 2097168 | tf_op jit(solution)/shard_map/psum | solution.py:115
  333.6 16.0 %convolution_bitcast_fusion.4 = f32[3,1024,128]{2,1,0:T(8,128)} fusion(bf16[4096,3,1024]{2,0,1:T(8,128)(2,1)} %param.18, f32[4096,128]{0,1:T(8,128)} %all-reduce.14.cloned.1.call-done), kind=kOutput, calls=%fused_computation.12 | convolution fusion | flops 3221749760 | bytes 28835840 | tf_op jit(solution)/shard_map/dot_general | solution.py:119
  352.4 6.5 %collective-permute-done.11 = f32[512,128]{1,0:T(8,128)S(1)} collective-permute-done((f32[512,128]{1,0:T(8,128)S(1)}, f32[512,128]{1,0:T(8,128)S(1)}, u32[]{:S(2)}, u32[]{:S(2)}) %collective-permute-start.11) | collective-permute-done | bytes 262176 | tf_op jit(solution)/shard_map/ppermute | solution.py:11
  360.4 5.6 collective-permute-done.12
  366.1 4.9 convolution_bitcast_fusion.3
  371.0 36.6 %all-reduce.16.cloned.1.call-done = f32[2048,128]{0,1:T(8,128)} async-done(((f32[2048,128]{0,1:T(8,128)}), f32[2048,128]{0,1:T(8,128)}) %all-reduce.16.cloned.1.call-update) | async-done | bytes 1048592 | tf_op jit(solution)/shard_map/psum | solution.py:115
  407.6 7.6 %fusion.6 = f32[2,1024,128]{2,1,0:T(8,128)S(1)} fusion(bf16[2048,2,1024]{2,1,0:T(2,128)(2,1)} %param.17, f32[2048,128]{0,1:T(8,128)} %all-reduce.16.cloned.1.call-done), kind=kOutput, calls=%fused_computation.13 | convolution fusion | flops 1074003968 | bytes 10485760 | tf_op jit(solution)/shard_map/dot_general | solution.py:119
  418.3 6.4 %collective-permute-done.13 = f32[512,128]{1,0:T(8,128)S(1)} collective-permute-done((f32[512,128]{1,0:T(8,128)S(1)}, f32[512,128]{1,0:T(8,128)S(1)}, u32[]{:S(2)}, u32[]{:S(2)}) %collective-permute-start.13) | collective-permute-done | bytes 262176 | tf_op jit(solution)/shard_map/ppermute | solution.py:11
  426.0 3.7 collective-permute-done.14
  431.1 3.7 collective-permute-done.15
  436.1 5.1 collective-permute-done.16
  443.3 33.5 %all-reduce.18.cloned.1.call-done = f32[1024,128]{0,1:T(8,128)} async-done(((f32[1024,128]{0,1:T(8,128)}), f32[1024,128]{0,1:T(8,128)}) %all-reduce.18.cloned.1.call-update) | async-done | bytes 524304 | tf_op jit(solution)/shard_map/psum | solution.py:115
  476.8 2.9 fusion.15
  481.3 5.4 collective-permute-done.17
  488.5 3.2 collective-permute-done.18
  491.7 3.3 collective-permute-start.19
  495.0 4.4 collective-permute-done.19
  501.4 3.1 collective-permute-done.20
  511.8 2.9 convolution_bitcast_fusion.6
  516.8 39.7 %psum.63 = f32[]{:T(128)} all-reduce(f32[]{:T(128)S(6)} %add.189), channel_id=1, replica_groups=mesh['leaf'=8,'rows'=4] {'leaf','rows'}, use_global_device_ids=true, to_apply=%region_12.13 | all-reduce | flops 1 | bytes 8 | tf_op jit(solution)/shard_map/psum | solution.py:97
  557.2 2.9 copy.60
  560.1 2.6 copy.59
  (104 shorter events, 44.2 us)
Async XLA Ops:
  7.2 73.2 %copy-start = (bf16[1024,1024]{1,0:T(8,128)(2,1)S(1)}, bf16[1024,1024]{1,0:T(8,128)(2,1)}, u32[]{:S(2)}) copy-start(bf16[1024,1024]{1,0:T(8,128)(2,1)} %param.13) | copy-start | bytes 6291460
  7.2 73.2 %all-reduce.8.cloned.1.call-start = ((), (), s32[]{:S(2)}) async-start(), calls=%async_computation | async-start | bytes 1048576 | tf_op jit(solution)/shard_map/psum | solution.py:84
  9.1 9.3 %collective-permute-start = (f32[512,128]{1,0:T(8,128)S(1)}, f32[512,128]{1,0:T(8,128)S(1)}, u32[]{:S(2)}, u32[]{:S(2)}) collective-permute-start(f32[512,128]{1,0:T(8,128)S(1)} %constant_dynamic-slice_fusion.5), channel_id=1, source_target_pairs={{0,4},{4,0},{8,12},{12,8},{16,20},{20,16},{24,28},{28,24},{1,5},{5... | collective-permute-start | bytes 786440 | tf_op jit(solution)/shard_map/ppermute | solution.py:11
  18.5 5.0 collective-permute-start.1
  23.6 7.4 %collective-permute-start.2 = (f32[256,128]{1,0:T(8,128)S(1)}, f32[256,128]{1,0:T(8,128)S(1)}, u32[]{:S(2)}, u32[]{:S(2)}) collective-permute-start(f32[256,128]{1,0:T(8,128)S(1)} %dynamic-slice_add_fusion.5), channel_id=1, source_target_pairs={{0,16},{4,20},{8,24},{12,28},{16,0},{20,4},{24,8},{28,12},{1,17},{... | collective-permute-start | bytes 393224 | tf_op jit(solution)/shard_map/ppermute | solution.py:11
  31.0 5.0 collective-permute-start.3
  36.1 6.4 %collective-permute-start.4 = (f32[512,128]{1,0:T(8,128)S(1)}, f32[512,128]{1,0:T(8,128)S(1)}, u32[]{:S(2)}, u32[]{:S(2)}) collective-permute-start(f32[512,128]{1,0:T(8,128)S(1)} %maximum_select_fusion.6), channel_id=1, source_target_pairs={{0,4},{4,0},{8,12},{12,8},{16,20},{20,16},{24,28},{28,24},{1,5},{5... | collective-permute-start | bytes 786440 | tf_op jit(solution)/shard_map/ppermute | solution.py:11
  37.9 8.0 %copy-start.10 = (bf16[1024,128]{1,0:T(8,128)(2,1)S(1)}, bf16[1024,128]{1,0:T(8,128)(2,1)}, u32[]{:S(2)}) copy-start(bf16[1024,128]{1,0:T(8,128)(2,1)} %param.20) | copy-start | bytes 786436
  42.5 3.4 copy-start.7
  45.9 108.8 %all-reduce.10.cloned.1.call-start = ((), (), s32[]{:S(2)}) async-start(), calls=%async_computation.1 | async-start | bytes 2097152 | tf_op jit(solution)/shard_map/psum | solution.py:84
  82.4 6.9 %collective-permute-start.5 = (f32[512,128]{1,0:T(8,128)S(1)}, f32[512,128]{1,0:T(8,128)S(1)}, u32[]{:S(2)}, u32[]{:S(2)}) collective-permute-start(f32[512,128]{1,0:T(8,128)S(1)} %dynamic-slice_bitcast_fusion.3), channel_id=1, source_target_pairs={{0,4},{4,0},{8,12},{12,8},{16,20},{20,16},{24,28},{28,24},{1,5},{5... | collective-permute-start | bytes 786440 | tf_op jit(solution)/shard_map/ppermute | solution.py:11
  89.4 5.5 collective-permute-start.6
  94.9 5.0 collective-permute-start.7
  100.0 12.0 %copy-start.1 = (f32[512,128]{1,0:T(8,128)}, f32[512,128]{1,0:T(8,128)S(1)}, u32[]{:S(2)}) copy-start(f32[512,128]{1,0:T(8,128)S(1)} %maximum_select_fusion.7) | copy-start | bytes 786436
  100.0 12.0 %collective-permute-start.8 = (f32[512,128]{1,0:T(8,128)S(1)}, f32[512,128]{1,0:T(8,128)S(1)}, u32[]{:S(2)}, u32[]{:S(2)}) collective-permute-start(f32[512,128]{1,0:T(8,128)S(1)} %maximum_select_fusion.7), channel_id=1, source_target_pairs={{0,4},{4,0},{8,12},{12,8},{16,20},{20,16},{24,28},{28,24},{1,5},{5... | collective-permute-start | bytes 786440 | tf_op jit(solution)/shard_map/ppermute | solution.py:11
  111.9 7.4 %copy-start.8 = (f32[512,128]{1,0:T(8,128)}, f32[512,128]{1,0:T(8,128)S(1)}, u32[]{:S(2)}) copy-start(f32[512,128]{1,0:T(8,128)S(1)} %collective-permute-done.8) | copy-start | bytes 786436
  119.3 147.6 %all-reduce.12.cloned.1.call-start = ((), (), s32[]{:S(2)}) async-start(), calls=%async_computation.2 | async-start | bytes 4194304 | tf_op jit(solution)/shard_map/psum | solution.py:84
  158.9 7.9 %collective-permute-start.9 = (f32[512,128]{1,0:T(8,128)S(1)}, f32[512,128]{1,0:T(8,128)S(1)}, u32[]{:S(2)}, u32[]{:S(2)}) collective-permute-start(f32[512,128]{1,0:T(8,128)S(1)} %dynamic-slice_bitcast_fusion.2), channel_id=1, source_target_pairs={{0,4},{4,0},{8,12},{12,8},{16,20},{20,16},{24,28},{28,24},{1,5},{5... | collective-permute-start | bytes 786440 | tf_op jit(solution)/shard_map/ppermute | solution.py:11
  166.9 34.7 %copy-start.3 = (f32[512,128]{1,0:T(8,128)}, f32[512,128]{1,0:T(8,128)S(1)}, u32[]{:S(2)}) copy-start(f32[512,128]{1,0:T(8,128)S(1)} %bitcast_add_fusion.2) | copy-start | bytes 786436
  166.9 34.7 %collective-permute-start.10 = (f32[512,128]{1,0:T(8,128)S(1)}, f32[512,128]{1,0:T(8,128)}, u32[]{:S(2)}, u32[]{:S(2)}) collective-permute-start(f32[512,128]{1,0:T(8,128)S(1)} %bitcast_add_fusion.2), channel_id=1, source_target_pairs={{0,4},{4,0},{8,12},{12,8},{16,20},{20,16},{24,28},{28,24},{1,5},{5... | collective-permute-start | bytes 786440 | tf_op jit(solution)/shard_map/ppermute | solution.py:11
  215.6 1.6 copy-start.11
  215.6 118.0 %all-reduce.14.cloned.1.call-start = ((), (), s32[]{:S(2)}) async-start(), calls=%async_computation.3 | async-start | bytes 4194304 | tf_op jit(solution)/shard_map/psum | solution.py:115
  282.0 125.6 %all-reduce.16.cloned.1.call-start = ((), (), s32[]{:S(2)}) async-start(), calls=%async_computation.4 | async-start | bytes 2097152 | tf_op jit(solution)/shard_map/psum | solution.py:115
  349.7 16.4 %copy-start.4 = (f32[512,128]{1,0:T(8,128)S(1)}, f32[512,128]{1,0:T(8,128)}, u32[]{:S(2)}) copy-start(f32[512,128]{1,0:T(8,128)} %copy-done.3) | copy-start | bytes 786436
  350.8 8.0 %collective-permute-start.11 = (f32[512,128]{1,0:T(8,128)S(1)}, f32[512,128]{1,0:T(8,128)S(1)}, u32[]{:S(2)}, u32[]{:S(2)}) collective-permute-start(f32[512,128]{1,0:T(8,128)S(1)} %dynamic-slice_bitcast_fusion.1), channel_id=1, source_target_pairs={{0,4},{4,0},{8,12},{12,8},{16,20},{20,16},{24,28},{28,24},{1,5},{5... | collective-permute-start | bytes 786440 | tf_op jit(solution)/shard_map/ppermute | solution.py:11
  358.9 7.2 %collective-permute-start.12 = (f32[512,128]{1,0:T(8,128)S(1)}, f32[512,128]{1,0:T(8,128)S(1)}, u32[]{:S(2)}, u32[]{:S(2)}) collective-permute-start(f32[512,128]{1,0:T(8,128)S(1)} %bitcast_add_fusion.1), channel_id=1, source_target_pairs={{0,4},{4,0},{8,12},{12,8},{16,20},{20,16},{24,28},{28,24},{1,5},{5... | collective-permute-start | bytes 786440 | tf_op jit(solution)/shard_map/ppermute | solution.py:11
  371.0 105.8 %all-reduce.18.cloned.1.call-start = ((), (), s32[]{:S(2)}) async-start(), calls=%async_computation.5 | async-start | bytes 1048576 | tf_op jit(solution)/shard_map/psum | solution.py:115
  415.1 14.6 %copy-start.6 = (f32[2,1024,128]{2,1,0:T(8,128)}, f32[2,1024,128]{2,1,0:T(8,128)S(1)}, u32[]{:S(2)}) copy-start(f32[2,1024,128]{2,1,0:T(8,128)S(1)} %fusion.6) | copy-start | bytes 3145732
  415.2 26.1 %copy-start.2 = (f32[512,128]{1,0:T(8,128)S(1)}, f32[512,128]{1,0:T(8,128)}, u32[]{:S(2)}) copy-start(f32[512,128]{1,0:T(8,128)} %copy-done.1) | copy-start | bytes 786436
  415.2 26.1 %copy-start.9 = (f32[512,128]{1,0:T(8,128)S(1)}, f32[512,128]{1,0:T(8,128)}, u32[]{:S(2)}) copy-start(f32[512,128]{1,0:T(8,128)} %copy-done.8) | copy-start | bytes 786436
  416.7 7.9 %collective-permute-start.13 = (f32[512,128]{1,0:T(8,128)S(1)}, f32[512,128]{1,0:T(8,128)S(1)}, u32[]{:S(2)}, u32[]{:S(2)}) collective-permute-start(f32[512,128]{1,0:T(8,128)S(1)} %dynamic-slice_bitcast_fusion), channel_id=1, source_target_pairs={{0,4},{4,0},{8,12},{12,8},{16,20},{20,16},{24,28},{28,24},{1,5},{5... | collective-permute-start | bytes 786440 | tf_op jit(solution)/shard_map/ppermute | solution.py:11
  424.7 5.0 collective-permute-start.14
  429.7 5.0 collective-permute-start.15
  434.8 6.4 %collective-permute-start.16 = (f32[512,128]{1,0:T(8,128)S(1)}, f32[512,128]{1,0:T(8,128)S(1)}, u32[]{:S(2)}, u32[]{:S(2)}) collective-permute-start(f32[512,128]{1,0:T(8,128)S(1)} %maximum_select_fusion.8), channel_id=1, source_target_pairs={{0,4},{4,0},{8,12},{12,8},{16,20},{20,16},{24,28},{28,24},{1,5},{5... | collective-permute-start | bytes 786440 | tf_op jit(solution)/shard_map/ppermute | solution.py:11
  443.0 120.7 %all-reduce.20.cloned.1.call-start = ((), (), s32[]{:S(2)}) async-start(), calls=%async_computation.6 | async-start | bytes 524288 | tf_op jit(solution)/shard_map/psum | solution.py:115
  479.7 6.9 %collective-permute-start.17 = (f32[512,128]{1,0:T(8,128)S(1)}, f32[512,128]{1,0:T(8,128)S(1)}, u32[]{:S(2)}, u32[]{:S(2)}) collective-permute-start(f32[512,128]{1,0:T(8,128)S(1)} %constant_dynamic-slice_fusion.1), channel_id=1, source_target_pairs={{0,4},{4,0},{8,12},{12,8},{16,20},{20,16},{24,28},{28,24},{1,5},{5... | collective-permute-start | bytes 786440 | tf_op jit(solution)/shard_map/ppermute | solution.py:11
  486.7 5.0 collective-permute-start.18
  491.7 7.6 %collective-permute-start.19 = (f32[256,128]{1,0:T(8,128)S(1)}, f32[256,128]{1,0:T(8,128)S(1)}, u32[]{:S(2)}, u32[]{:S(2)}) collective-permute-start(f32[256,128]{1,0:T(8,128)S(1)} %dynamic-slice_add_fusion.2), channel_id=1, source_target_pairs={{0,16},{4,20},{8,24},{12,28},{16,0},{20,4},{24,8},{28,12},{1,17},{... | collective-permute-start | bytes 393224 | tf_op jit(solution)/shard_map/ppermute | solution.py:11
  499.4 5.0 collective-permute-start.20
  505.1 6.7 %collective-permute-start.21 = (f32[512,128]{1,0:T(8,128)}, f32[512,128]{1,0:T(8,128)}, u32[]{:S(2)}, u32[]{:S(2)}) collective-permute-start(f32[512,128]{1,0:T(8,128)} %maximum_select_fusion.9), channel_id=1, source_target_pairs={{0,4},{4,0},{8,12},{12,8},{16,20},{20,16},{24,28},{28,24},{1,5},{5... | collective-permute-start | bytes 786440 | tf_op jit(solution)/shard_map/ppermute | solution.py:11
  560.1 2.6 copy-start.5
Sparse Core Ops, SparseCore 0:
  46.0 34.3 all-reduce.7
  119.5 35.1 all-reduce.9
  215.7 51.1 all-reduce.11
  282.1 51.4 all-reduce.13
  371.1 36.4 all-reduce.15
  443.1 33.6 all-reduce.17
  514.9 31.7 all-reduce.19
where the time goes:
time: 575 us; the launch traced here: 573 us
  waiting for transfers between devices  329 us (57%)
  matrix products  82.6 us (14%)
  local copies, waits for them, and re-layouts  56.1 us (10%)
  blocking collectives  39.7 us (7%)
  starting transfers between devices  37.8 us (7%)
  between operations  18.8 us (3%)
  other arithmetic  9.3 us (2%)
    psum x4, waiting for transfers between devices, on_device(): solved_exact = lax.psum(solved_terms, 'rows')  121 us
    psum x3, waiting for transfers between devices, on_device(): right_side = right_side - lax.psum(ancestor_terms, 'rows')  118 us
    ppermute x22, waiting for transfers between devices, swapped(): lax.ppermute(x, axis, [(i, i ^ 1 << apart) for i in range(lax.axis_size(a...  89.8 us
    unnamed x33, local copies, waits for them, and re-layouts  54.7 us
    psum x1, blocking collectives, on_device(): loss_total = lax.psum(loss_sum, ('leaf', 'rows'))  39.7 us
    ppermute x22, starting transfers between devices, swapped(): lax.ppermute(x, axis, [(i, i ^ 1 << apart) for i in range(lax.axis_size(a...  36.9 us
    dot_general x3, matrix products, on_device(): lax.dot_general(couplings[tree_level], solved, contract_rows, preferred_e...  26.5 us
    dot_general x3, matrix products, on_device(): jnp.dot(flat_coupling, stacked, preferred_element_type=jnp.float32)  23.5 us
  transfers between devices with their start and end apart: 29, of which 26 were waited for; matrix products, arithmetic and copies ran while one was open for 10% of the time, Pallas kernels for 0%

commit v1 on v0

--- a/solution.py
+++ b/solution.py
@@ -81,7 +81,7 @@
             )
             stacked = jnp.concatenate(rounded, axis=0)
             ancestor_terms = jnp.dot(flat_coupling, stacked, preferred_element_type=jnp.float32)
-            right_side = right_side - lax.psum(ancestor_terms, "rows")
+            right_side = right_side - jnp.sum(lax.all_gather(ancestor_terms, "rows"), axis=0)
         right_round = right_side.astype(jnp.bfloat16)
         partial_sample = lax.dot_general(
             factors[tree_level], right_round, contract_rows, preferred_element_type=jnp.float32

time: 575 us -> 617 us (1.073); the launches traced: 573 us -> 607 us
  local copies, waits for them, and re-layouts: 56.1 us -> 77.9 us
  other arithmetic: 9.3 us -> 26 us
    psum x3 -> x0, waiting for transfers between devices: 118 us -> none  [on_device(): right_side = right_side - lax.psum(ancestor_terms, 'rows')]
    all_gather x0 -> x3, waiting for transfers between devices: none -> 112 us  [on_device(): lax.all_gather(ancestor_terms, 'rows')]
    all_gather x0 -> x3, local copies, waits for them, and re-layouts: none -> 20.5 us  [on_device(): lax.all_gather(ancestor_terms, 'rows')]
    reduce_sum x0 -> x3, other arithmetic: none -> 17.7 us  [on_device(): jnp.sum(lax.all_gather(ancestor_terms, 'rows'), axis=0)]
    unnamed x33 -> x45, local copies, waits for them, and re-layouts: 54.7 us -> 56 us
where the time goes in v1:
time: 617 us; the launch traced here: 607 us
  waiting for transfers between devices  325 us (53%)
  matrix products  81.1 us (13%)
  local copies, waits for them, and re-layouts  77.9 us (13%)
  blocking collectives  39.7 us (6%)
  starting transfers between devices  37.7 us (6%)
  other arithmetic  26 us (4%)
  between operations  19 us (3%)
    psum x4, waiting for transfers between devices, on_device(): solved_exact = lax.psum(solved_terms, 'rows')  121 us
    all_gather x3, waiting for transfers between devices, on_device(): lax.all_gather(ancestor_terms, 'rows')  112 us
    ppermute x22, waiting for transfers between devices, swapped(): lax.ppermute(x, axis, [(i, i ^ 1 << apart) for i in range(lax.axis_size(a...  92.1 us
    unnamed x45, local copies, waits for them, and re-layouts  56 us
    psum x1, blocking collectives, on_device(): loss_total = lax.psum(loss_sum, ('leaf', 'rows'))  39.7 us
    ppermute x22, starting transfers between devices, swapped(): lax.ppermute(x, axis, [(i, i ^ 1 << apart) for i in range(lax.axis_size(a...  36.3 us
    dot_general x3, matrix products, on_device(): lax.dot_general(couplings[tree_level], solved, contract_rows, preferred_e...  26.5 us
    dot_general x3, matrix products, on_device(): jnp.dot(flat_coupling, stacked, preferred_element_type=jnp.float32)  23.5 us
  transfers between devices with their start and end apart: 29, of which 26 were waited for; matrix products, arithmetic and copies ran while one was open for 10% of the time, Pallas kernels for 0%

profile of v1, /device:TPU:0, one launch (start us, length us, event | category | flops | bytes accessed | tf_op | source)
XLA Modules:
  0.0 606.6 jit_solution(7835162208882671189)
XLA Ops:
  9.1 3.0 collective-permute-start
  12.1 6.3 %collective-permute-done = f32[512,128]{1,0:T(8,128)S(1)} collective-permute-done((f32[512,128]{1,0:T(8,128)S(1)}, f32[512,128]{1,0:T(8,128)S(1)}, u32[]{:S(2)}, u32[]{:S(2)}) %collective-permute-start) | collective-permute-done | bytes 262176 | tf_op jit(solution)/shard_map/ppermute | solution.py:11
  20.4 3.2 collective-permute-done.1
  26.3 4.7 collective-permute-done.2
  31.7 4.3 collective-permute-done.3
  37.9 4.6 collective-permute-done.4
  42.6 3.3 fusion.9
  46.1 23.7 %all-gather.7.cloned.1.call-done = f32[4096,128]{0,1:T(8,128)} async-done(((f32[1024,128]{0,1:T(8,128)}), f32[4096,128]{0,1:T(8,128)}) %all-gather.7.cloned.1.call-update) | async-done | bytes 2097168 | tf_op jit(solution)/shard_map/all_gather | solution.py:84
  69.8 3.6 reshape.35
  73.4 2.9 reduce_sum.73
  78.8 7.0 %collective-permute-done.5 = f32[512,128]{1,0:T(8,128)S(1)} collective-permute-done((f32[512,128]{1,0:T(8,128)S(1)}, f32[512,128]{1,0:T(8,128)S(1)}, u32[]{:S(2)}, u32[]{:S(2)}) %collective-permute-start.5) | collective-permute-done | bytes 262176 | tf_op jit(solution)/shard_map/ppermute | solution.py:11
  87.4 3.5 collective-permute-done.6
  92.4 3.5 collective-permute-done.7
  97.5 10.2 %copy.84 = bf16[256,8,2,1024]{3,1,2,0:T(8,128)(2,1)} copy(bf16[256,8,2,1024]{3,2,1,0:T(2,128)(2,1)} %bitcast.85) | data formatting | bytes 16777216
  109.1 7.3 %convolution_bitcast_fusion.2 = f32[2048,128]{0,1:T(8,128)} fusion(bf16[2048,2048]{1,0:T(8,128)(2,1)} %bitcast.84, bf16[1024,128]{1,0:T(8,128)(2,1)S(1)} %fusion.44, bf16[1024,128]{1,0:T(8,128)(2,1)S(1)} %fusion.45), kind=kOutput, calls=%fused_computation.4 | convolution fusion | flops 1074790400 | bytes 9961472 | tf_op jit(solution)/shard_map/dot_general | solution.py:83
  117.7 32.5 %all-gather.9.cloned.1.call-done = f32[8192,128]{0,1:T(8,128)} async-done(((f32[2048,128]{0,1:T(8,128)}), f32[8192,128]{0,1:T(8,128)}) %all-gather.9.cloned.1.call-update) | async-done | bytes 4194320 | tf_op jit(solution)/shard_map/all_gather | solution.py:84
  150.2 6.1 %reshape.36 = f32[4,2048,128]{1,0,2:T(4,128)} reshape(f32[8192,128]{0,1:T(8,128)} %all-gather.9.cloned.1.call-done) | data formatting | bytes 8388608 | tf_op jit(solution)/shard_map/all_gather | solution.py:84
  156.3 4.8 reduce_sum.74
  161.2 4.1 fusion.26
  166.8 7.0 %collective-permute-done.9 = f32[512,128]{1,0:T(8,128)S(1)} collective-permute-done((f32[512,128]{1,0:T(8,128)S(1)}, f32[512,128]{1,0:T(8,128)S(1)}, u32[]{:S(2)}, u32[]{:S(2)}) %collective-permute-start.9) | collective-permute-done | bytes 262176 | tf_op jit(solution)/shard_map/ppermute | solution.py:11
  175.4 33.6 %copy.68 = bf16[4096,3,1024]{0,2,1:T(8,128)(2,1)} copy(bf16[4096,3,1024]{2,0,1:T(8,128)(2,1)} %param.18) | data formatting | bytes 50331648 | tf_op args[6]
  209.0 13.0 %convolution_bitcast_fusion.1 = f32[4096,128]{0,1:T(8,128)} fusion(bf16[4096,3072]{0,1:T(8,128)(2,1)} %bitcast.83, bf16[1024,128]{1,0:T(8,128)(2,1)S(1)} %fusion.42, bf16[1024,128]{1,0:T(8,128)(2,1)S(1)} %copy-done.2, bf16[1024,128]{1,0:T(8,128)(2,1)S(1)} %fusion.45), kind=kOutput, calls=%fused_computation.3 | convolution fusion | flops 3223584768 | bytes 28049408 | tf_op jit(solution)/shard_map/dot_general | solution.py:83
  223.9 55.7 %all-gather.11.cloned.1.call-done = f32[16384,128]{0,1:T(8,128)} async-done(((f32[4096,128]{0,1:T(8,128)}), f32[16384,128]{0,1:T(8,128)}) %all-gather.11.cloned.1.call-update) | async-done | bytes 8388624 | tf_op jit(solution)/shard_map/all_gather | solution.py:84
  279.6 10.8 %reshape.37 = f32[4,4096,128]{1,0,2:T(4,128)} reshape(f32[16384,128]{0,1:T(8,128)} %all-gather.11.cloned.1.call-done) | data formatting | bytes 16777216 | tf_op jit(solution)/shard_map/all_gather | solution.py:84
  290.3 10.0 %reduce_sum.75 = f32[4096,128]{0,1:T(8,128)} reduce(f32[4,4096,128]{1,0,2:T(4,128)} %reshape.37, f32[]{:T(128)} %constant.15.clone.1), dimensions={0}, to_apply=%region_3.4 | reduce | flops 1572864 | bytes 10485764 | tf_op jit(solution)/shard_map/reduce_sum | solution.py:84
  300.3 7.4 %fusion.28 = (f32[]{:T(128)}, f32[1024,128]{1,0:T(8,128)S(1)}) fusion(f32[128]{0:T(128)S(1)} %broadcast_add_fusion, bf16[4096,1024]{1,0:T(8,128)(2,1)} %param.15, f32[4096,128]{0,1:T(8,128)} %reduce_sum.75, bf16[4096,128]{0,1:T(8,128)(2,1)S(1)} %copy.61), kind=kOutput, calls=%fused_computation.32 | convolution fusion | flops 1076494336 | bytes 12059140 | tf_op jit(solution)/shard_map/dot_general | solution.py:86
  307.8 7.6 %convolution_bitcast_fusion = f32[4096,128]{0,1:T(8,128)} fusion(bf16[4096,1024]{1,0:T(8,128)(2,1)} %param.15, f32[1024,128]{1,0:T(8,128)S(1)} %get-tuple-element.26, f32[128]{0:T(128)S(1)} %broadcast_add_fusion), kind=kOutput, calls=%fused_computation.2 | convolution fusion | flops 1074397184 | bytes 11010560 | tf_op jit(solution)/shard_map/dot_general | solution.py:112
  315.7 51.2 %all-reduce.5.cloned.1.call-done = f32[4096,128]{0,1:T(8,128)} async-done(((f32[4096,128]{0,1:T(8,128)}), f32[4096,128]{0,1:T(8,128)}) %all-reduce.5.cloned.1.call-update) | async-done | bytes 2097168 | tf_op jit(solution)/shard_map/psum | solution.py:115
  367.0 16.0 %convolution_bitcast_fusion.4 = f32[3,1024,128]{2,1,0:T(8,128)} fusion(bf16[4096,3,1024]{2,0,1:T(8,128)(2,1)} %param.18, f32[4096,128]{0,1:T(8,128)} %all-reduce.5.cloned.1.call-done), kind=kOutput, calls=%fused_computation.12 | convolution fusion | flops 3221749760 | bytes 28835840 | tf_op jit(solution)/shard_map/dot_general | solution.py:119
  385.7 6.5 %collective-permute-done.11 = f32[512,128]{1,0:T(8,128)S(1)} collective-permute-done((f32[512,128]{1,0:T(8,128)S(1)}, f32[512,128]{1,0:T(8,128)S(1)}, u32[]{:S(2)}, u32[]{:S(2)}) %collective-permute-start.11) | collective-permute-done | bytes 262176 | tf_op jit(solution)/shard_map/ppermute | solution.py:11
  393.8 5.6 collective-permute-done.12
  399.4 4.7 convolution_bitcast_fusion.3
  404.2 36.6 %all-reduce.7.cloned.1.call-done = f32[2048,128]{0,1:T(8,128)} async-done(((f32[2048,128]{0,1:T(8,128)}), f32[2048,128]{0,1:T(8,128)}) %all-reduce.7.cloned.1.call-update) | async-done | bytes 1048592 | tf_op jit(solution)/shard_map/psum | solution.py:115
  440.7 7.6 %fusion.6 = f32[2,1024,128]{2,1,0:T(8,128)S(1)} fusion(bf16[2048,2,1024]{2,1,0:T(2,128)(2,1)} %param.17, f32[2048,128]{0,1:T(8,128)} %all-reduce.7.cloned.1.call-done), kind=kOutput, calls=%fused_computation.13 | convolution fusion | flops 1074003968 | bytes 10485760 | tf_op jit(solution)/shard_map/dot_general | solution.py:119
  451.4 6.4 %collective-permute-done.13 = f32[512,128]{1,0:T(8,128)S(1)} collective-permute-done((f32[512,128]{1,0:T(8,128)S(1)}, f32[512,128]{1,0:T(8,128)S(1)}, u32[]{:S(2)}, u32[]{:S(2)}) %collective-permute-start.13) | collective-permute-done | bytes 262176 | tf_op jit(solution)/shard_map/ppermute | solution.py:11
  459.1 3.7 collective-permute-done.14
  464.2 3.7 collective-permute-done.15
  469.2 5.1 collective-permute-done.16
  476.6 33.3 %all-reduce.9.cloned.1.call-done = f32[1024,128]{0,1:T(8,128)} async-done(((f32[1024,128]{0,1:T(8,128)}), f32[1024,128]{0,1:T(8,128)}) %all-reduce.9.cloned.1.call-update) | async-done | bytes 524304 | tf_op jit(solution)/shard_map/psum | solution.py:115
  509.9 2.9 fusion.15
  514.4 5.4 collective-permute-done.17
  521.7 3.2 collective-permute-done.18
  524.9 3.3 collective-permute-start.19
  528.2 4.3 collective-permute-done.19
  534.5 3.1 collective-permute-done.20
  545.0 2.8 convolution_bitcast_fusion.6
  549.8 39.7 %psum.39 = f32[]{:T(128)} all-reduce(f32[]{:T(128)S(6)} %add.183), channel_id=1, replica_groups=mesh['leaf'=8,'rows'=4] {'leaf','rows'}, use_global_device_ids=true, to_apply=%region_12.13 | all-reduce | flops 1 | bytes 8 | tf_op jit(solution)/shard_map/psum | solution.py:97
  590.2 2.9 copy.77
  (122 shorter events, 56.0 us)
Async XLA Ops:
  7.2 69.1 %copy-start = (bf16[1024,1024]{1,0:T(8,128)(2,1)S(1)}, bf16[1024,1024]{1,0:T(8,128)(2,1)}, u32[]{:S(2)}) copy-start(bf16[1024,1024]{1,0:T(8,128)(2,1)} %param.13) | copy-start | bytes 6291460
  7.2 62.6 %all-gather.7.cloned.1.call-start = ((), (), s32[]{:S(2)}) async-start(), calls=%async_computation.4 | async-start | bytes 2621440 | tf_op jit(solution)/shard_map/all_gather | solution.py:84
  9.1 9.3 %collective-permute-start = (f32[512,128]{1,0:T(8,128)S(1)}, f32[512,128]{1,0:T(8,128)S(1)}, u32[]{:S(2)}, u32[]{:S(2)}) collective-permute-start(f32[512,128]{1,0:T(8,128)S(1)} %constant_dynamic-slice_fusion.5), channel_id=1, source_target_pairs={{0,4},{4,0},{8,12},{12,8},{16,20},{20,16},{24,28},{28,24},{1,5},{5... | collective-permute-start | bytes 786440 | tf_op jit(solution)/shard_map/ppermute | solution.py:11
  18.5 5.0 collective-permute-start.1
  23.6 7.4 %collective-permute-start.2 = (f32[256,128]{1,0:T(8,128)S(1)}, f32[256,128]{1,0:T(8,128)S(1)}, u32[]{:S(2)}, u32[]{:S(2)}) collective-permute-start(f32[256,128]{1,0:T(8,128)S(1)} %dynamic-slice_add_fusion.5), channel_id=1, source_target_pairs={{0,16},{4,20},{8,24},{12,28},{16,0},{20,4},{24,8},{28,12},{1,17},{... | collective-permute-start | bytes 393224 | tf_op jit(solution)/shard_map/ppermute | solution.py:11
  31.0 5.0 collective-permute-start.3
  36.1 9.8 %copy-start.3 = (f32[512,128]{1,0:T(8,128)}, f32[512,128]{1,0:T(8,128)S(1)}, u32[]{:S(2)}) copy-start(f32[512,128]{1,0:T(8,128)S(1)} %maximum_select_fusion.6) | copy-start | bytes 786436
  36.1 6.4 %collective-permute-start.4 = (f32[512,128]{1,0:T(8,128)S(1)}, f32[512,128]{1,0:T(8,128)S(1)}, u32[]{:S(2)}, u32[]{:S(2)}) collective-permute-start(f32[512,128]{1,0:T(8,128)S(1)} %maximum_select_fusion.6), channel_id=1, source_target_pairs={{0,4},{4,0},{8,12},{12,8},{16,20},{20,16},{24,28},{28,24},{1,5},{5... | collective-permute-start | bytes 786440 | tf_op jit(solution)/shard_map/ppermute | solution.py:11
  37.9 8.0 %copy-start.16 = (bf16[1024,128]{1,0:T(8,128)(2,1)S(1)}, bf16[1024,128]{1,0:T(8,128)(2,1)}, u32[]{:S(2)}) copy-start(bf16[1024,128]{1,0:T(8,128)(2,1)} %param.20) | copy-start | bytes 786436
  42.5 3.4 copy-start.9
  45.9 104.3 %all-gather.9.cloned.1.call-start = ((), (), s32[]{:S(2)}) async-start(), calls=%async_computation.5 | async-start | bytes 5242880 | tf_op jit(solution)/shard_map/all_gather | solution.py:84
  77.3 8.5 %collective-permute-start.5 = (f32[512,128]{1,0:T(8,128)S(1)}, f32[512,128]{1,0:T(8,128)S(1)}, u32[]{:S(2)}, u32[]{:S(2)}) collective-permute-start(f32[512,128]{1,0:T(8,128)S(1)} %dynamic-slice_bitcast_fusion.3), channel_id=1, source_target_pairs={{0,4},{4,0},{8,12},{12,8},{16,20},{20,16},{24,28},{28,24},{1,5},{5... | collective-permute-start | bytes 786440 | tf_op jit(solution)/shard_map/ppermute | solution.py:11
  85.8 5.0 collective-permute-start.6
  90.9 5.0 collective-permute-start.7
  96.0 11.7 %copy-start.5 = (f32[512,128]{1,0:T(8,128)}, f32[512,128]{1,0:T(8,128)S(1)}, u32[]{:S(2)}) copy-start(f32[512,128]{1,0:T(8,128)S(1)} %maximum_select_fusion.7) | copy-start | bytes 786436
  96.0 11.7 %collective-permute-start.8 = (f32[512,128]{1,0:T(8,128)S(1)}, f32[512,128]{1,0:T(8,128)S(1)}, u32[]{:S(2)}, u32[]{:S(2)}) collective-permute-start(f32[512,128]{1,0:T(8,128)S(1)} %maximum_select_fusion.7), channel_id=1, source_target_pairs={{0,4},{4,0},{8,12},{12,8},{16,20},{20,16},{24,28},{28,24},{1,5},{5... | collective-permute-start | bytes 786440 | tf_op jit(solution)/shard_map/ppermute | solution.py:11
  107.7 0.7 copy-start.11
  108.4 0.7 copy-start.1
  109.1 7.6 %copy-start.15 = (bf16[2048,128]{1,0:T(8,128)(2,1)S(1)}, bf16[2048,128]{1,0:T(8,128)(2,1)}, u32[]{:S(2)}) copy-start(bf16[2048,128]{1,0:T(8,128)(2,1)} %param.21) | copy-start | bytes 1572868
  116.5 163.1 %all-gather.11.cloned.1.call-start = ((), (), s32[]{:S(2)}) async-start(), calls=%async_computation.6 | async-start | bytes 10485760 | tf_op jit(solution)/shard_map/all_gather | solution.py:84
  165.3 8.5 %collective-permute-start.9 = (f32[512,128]{1,0:T(8,128)S(1)}, f32[512,128]{1,0:T(8,128)S(1)}, u32[]{:S(2)}, u32[]{:S(2)}) collective-permute-start(f32[512,128]{1,0:T(8,128)S(1)} %dynamic-slice_bitcast_fusion.2), channel_id=1, source_target_pairs={{0,4},{4,0},{8,12},{12,8},{16,20},{20,16},{24,28},{28,24},{1,5},{5... | collective-permute-start | bytes 786440 | tf_op jit(solution)/shard_map/ppermute | solution.py:11
  173.8 35.2 %copy-start.2 = (bf16[1024,128]{1,0:T(8,128)(2,1)S(1)}, bf16[1024,128]{1,0:T(8,128)(2,1)}, u32[]{:S(2)}) copy-start(bf16[1024,128]{1,0:T(8,128)(2,1)} %copy-done.1) | copy-start | bytes 786436
  173.9 35.1 %collective-permute-start.10 = (f32[512,128]{1,0:T(8,128)S(1)}, f32[512,128]{1,0:T(8,128)S(1)}, u32[]{:S(2)}, u32[]{:S(2)}) collective-permute-start(f32[512,128]{1,0:T(8,128)S(1)} %bitcast_add_fusion.2), channel_id=1, source_target_pairs={{0,4},{4,0},{8,12},{12,8},{16,20},{20,16},{24,28},{28,24},{1,5},{5... | collective-permute-start | bytes 786440 | tf_op jit(solution)/shard_map/ppermute | solution.py:11
  209.0 13.0 %copy-start.13 = (f32[512,128]{1,0:T(8,128)}, f32[512,128]{1,0:T(8,128)S(1)}, u32[]{:S(2)}) copy-start(f32[512,128]{1,0:T(8,128)S(1)} %collective-permute-done.10) | copy-start | bytes 786436
  222.0 1.8 copy-start.17
  222.0 144.9 %all-reduce.5.cloned.1.call-start = ((), (), s32[]{:S(2)}) async-start(), calls=%async_computation | async-start | bytes 4194304 | tf_op jit(solution)/shard_map/psum | solution.py:115
  315.4 125.3 %all-reduce.7.cloned.1.call-start = ((), (), s32[]{:S(2)}) async-start(), calls=%async_computation.1 | async-start | bytes 2097152 | tf_op jit(solution)/shard_map/psum | solution.py:115
  383.0 16.4 %copy-start.14 = (f32[512,128]{1,0:T(8,128)S(1)}, f32[512,128]{1,0:T(8,128)}, u32[]{:S(2)}) copy-start(f32[512,128]{1,0:T(8,128)} %copy-done.13) | copy-start | bytes 786436
  384.2 8.0 %collective-permute-start.11 = (f32[512,128]{1,0:T(8,128)S(1)}, f32[512,128]{1,0:T(8,128)S(1)}, u32[]{:S(2)}, u32[]{:S(2)}) collective-permute-start(f32[512,128]{1,0:T(8,128)S(1)} %dynamic-slice_bitcast_fusion.1), channel_id=1, source_target_pairs={{0,4},{4,0},{8,12},{12,8},{16,20},{20,16},{24,28},{28,24},{1,5},{5... | collective-permute-start | bytes 786440 | tf_op jit(solution)/shard_map/ppermute | solution.py:11
  392.2 7.2 %collective-permute-start.12 = (f32[512,128]{1,0:T(8,128)S(1)}, f32[512,128]{1,0:T(8,128)S(1)}, u32[]{:S(2)}, u32[]{:S(2)}) collective-permute-start(f32[512,128]{1,0:T(8,128)S(1)} %bitcast_add_fusion.1), channel_id=1, source_target_pairs={{0,4},{4,0},{8,12},{12,8},{16,20},{20,16},{24,28},{28,24},{1,5},{5... | collective-permute-start | bytes 786440 | tf_op jit(solution)/shard_map/ppermute | solution.py:11
  404.1 105.8 %all-reduce.9.cloned.1.call-start = ((), (), s32[]{:S(2)}) async-start(), calls=%async_computation.2 | async-start | bytes 1048576 | tf_op jit(solution)/shard_map/psum | solution.py:115
  448.3 14.6 %copy-start.8 = (f32[2,1024,128]{2,1,0:T(8,128)}, f32[2,1024,128]{2,1,0:T(8,128)S(1)}, u32[]{:S(2)}) copy-start(f32[2,1024,128]{2,1,0:T(8,128)S(1)} %fusion.6) | copy-start | bytes 3145732
  448.3 26.1 %copy-start.6 = (f32[512,128]{1,0:T(8,128)S(1)}, f32[512,128]{1,0:T(8,128)}, u32[]{:S(2)}) copy-start(f32[512,128]{1,0:T(8,128)} %copy-done.5) | copy-start | bytes 786436
  448.3 26.1 %copy-start.12 = (f32[512,128]{1,0:T(8,128)S(1)}, f32[512,128]{1,0:T(8,128)}, u32[]{:S(2)}) copy-start(f32[512,128]{1,0:T(8,128)} %copy-done.11) | copy-start | bytes 786436
  449.9 7.9 %collective-permute-start.13 = (f32[512,128]{1,0:T(8,128)S(1)}, f32[512,128]{1,0:T(8,128)S(1)}, u32[]{:S(2)}, u32[]{:S(2)}) collective-permute-start(f32[512,128]{1,0:T(8,128)S(1)} %dynamic-slice_bitcast_fusion), channel_id=1, source_target_pairs={{0,4},{4,0},{8,12},{12,8},{16,20},{20,16},{24,28},{28,24},{1,5},{5... | collective-permute-start | bytes 786440 | tf_op jit(solution)/shard_map/ppermute | solution.py:11
  457.8 5.0 collective-permute-start.14
  462.9 5.0 collective-permute-start.15
  467.9 6.4 %collective-permute-start.16 = (f32[512,128]{1,0:T(8,128)S(1)}, f32[512,128]{1,0:T(8,128)S(1)}, u32[]{:S(2)}, u32[]{:S(2)}) collective-permute-start(f32[512,128]{1,0:T(8,128)S(1)} %maximum_select_fusion.8), channel_id=1, source_target_pairs={{0,4},{4,0},{8,12},{12,8},{16,20},{20,16},{24,28},{28,24},{1,5},{5... | collective-permute-start | bytes 786440 | tf_op jit(solution)/shard_map/ppermute | solution.py:11
  476.1 120.6 %all-reduce.11.cloned.1.call-start = ((), (), s32[]{:S(2)}) async-start(), calls=%async_computation.3 | async-start | bytes 524288 | tf_op jit(solution)/shard_map/psum | solution.py:115
  512.8 20.0 %copy-start.4 = (f32[512,128]{1,0:T(8,128)S(1)}, f32[512,128]{1,0:T(8,128)}, u32[]{:S(2)}) copy-start(f32[512,128]{1,0:T(8,128)} %copy-done.3) | copy-start | bytes 786436
  512.9 6.9 %collective-permute-start.17 = (f32[512,128]{1,0:T(8,128)S(1)}, f32[512,128]{1,0:T(8,128)S(1)}, u32[]{:S(2)}, u32[]{:S(2)}) collective-permute-start(f32[512,128]{1,0:T(8,128)S(1)} %constant_dynamic-slice_fusion.1), channel_id=1, source_target_pairs={{0,4},{4,0},{8,12},{12,8},{16,20},{20,16},{24,28},{28,24},{1,5},{5... | collective-permute-start | bytes 786440 | tf_op jit(solution)/shard_map/ppermute | solution.py:11
  519.8 5.0 collective-permute-start.18
  524.9 7.6 %collective-permute-start.19 = (f32[256,128]{1,0:T(8,128)S(1)}, f32[256,128]{1,0:T(8,128)S(1)}, u32[]{:S(2)}, u32[]{:S(2)}) collective-permute-start(f32[256,128]{1,0:T(8,128)S(1)} %dynamic-slice_add_fusion.2), channel_id=1, source_target_pairs={{0,16},{4,20},{8,24},{12,28},{16,0},{20,4},{24,8},{28,12},{1,17},{... | collective-permute-start | bytes 393224 | tf_op jit(solution)/shard_map/ppermute | solution.py:11
  528.2 16.8 %copy-start.10 = (f32[512,128]{1,0:T(8,128)S(1)}, f32[512,128]{1,0:T(8,128)}, u32[]{:S(2)}) copy-start(f32[512,128]{1,0:T(8,128)} %copy-done.9) | copy-start | bytes 786436
  532.5 5.0 collective-permute-start.20
  538.3 6.7 %collective-permute-start.21 = (f32[512,128]{1,0:T(8,128)}, f32[512,128]{1,0:T(8,128)}, u32[]{:S(2)}, u32[]{:S(2)}) collective-permute-start(f32[512,128]{1,0:T(8,128)} %maximum_select_fusion.9), channel_id=1, source_target_pairs={{0,4},{4,0},{8,12},{12,8},{16,20},{20,16},{24,28},{28,24},{1,5},{5... | collective-permute-start | bytes 786440 | tf_op jit(solution)/shard_map/ppermute | solution.py:11
  593.1 2.6 copy-start.7
Sparse Core Ops, SparseCore 0:
  46.0 23.7 all-gather.6
  116.6 33.5 all-gather.8
  222.1 57.3 all-gather.10
  315.5 51.3 all-reduce.4
  404.2 36.4 all-reduce.6
  476.2 33.6 all-reduce.8
  547.9 31.7 all-reduce.10
